TPU v7x, 512 devices: a whole 4x8x8 slice. The times are simulated.
512 devices in a mesh: mem: 4 (over x), lat: 4 (over y_hi, core), lon: 32 (over z, y_lo).
Axes of the slice: x: 4, y: 8 (y_hi: 2, y_lo: 4; y = y_hi * 4 + y_lo), z: 8, core: 2. Of those that a mesh axis runs over, the one named last changes fastest.
Arguments:
- initial_temp: float32 [100, 128, 512], P(None, 'lon', 'lat'), may hold values from -6 to 6
- land_mask: int32 [128, 512], P('lon', 'lat'), may hold values 0 or 1
- pert_table: float32 [16, 100], replicated, may hold values from 0.03 to 0.24
- pert_index: int32 [8], P('mem'), may hold values from 0 to 15
- base_kh: float32 [100], replicated, may hold values from 0.03 to 0.24
- member_mix: bfloat16 [8, 100, 100], P('mem'), may hold values from -0.15625 to 0.15625
- base_mix: bfloat16 [100, 100], replicated, may hold values from -0.15625 to 0.15625
- owner: int32 [32768, 1], P(('lat', 'lon')), may hold values from 0 to 127; in each aligned block of 256 rows (0 to 255, 256 to 511, ...) at most 4 rows name the same one
- column: int32 [32768], P(('lat', 'lon')), may hold values from 0 to 511
- interp_w: float32 [32768, 100], P(('lat', 'lon')), may hold values from 0 to 1
- obs_inv_var: float32 [32768, 100], P(('lat', 'lon')), may hold values from 1 to 16
- observed: float32 [32768, 100], P(('lat', 'lon')), may hold values from -6 to 6
Outputs:
- member_temp: bfloat16 [8, 100, 128, 512], P('mem', None, 'lon', 'lat')
- base_temp: bfloat16 [100, 128, 512], P(None, 'lon', 'lat')
- gram_block: float32 [8, 8], replicated
- projection: float32 [8], replicated
- misfit: float32 [32768, 100], P(('lat', 'lon'))
Inputs may be any that keep to these rules, and one draw needn't show every extreme that they name: Within the records of one device no owner is named more than 4 times, and in every draw some owner is named exactly 4 times by some device's records. The column within the owner's block is the longitude offset times 128 plus the latitude offset.
All inputs are finite; a program needn't handle non-finite values. No bound on the sum of `land_mask` on one device may be relied on, other than what follows from the above.
Results may differ from a plain program's by a relative error of at most 0.012.
Values may be sent and summed in bfloat16 or wider, within the bound.
No kernel may reach another device: no remote copies, remote signals or barrier semaphores. Data moves between devices by JAX's collectives and lax.ppermute only.
A program may use at most 64 MiB of HBM per device.

v0:
```python
import jax
import jax.numpy as jnp
from jax import lax
from jax.sharding import PartitionSpec as P

STEPS = 5


def padded_2(cells, sides, width, closed):
    for axis, dim in sides:
        count = lax.axis_size(axis)
        ends = count if closed else count - 1
        head = lax.slice_in_dim(cells, 0, width, axis=dim)
        tail = lax.slice_in_dim(cells, cells.shape[dim] - width, cells.shape[dim], axis=dim)
        cells = jnp.concatenate(
            [
                lax.ppermute(tail, axis, [(i, (i + 1) % count) for i in range(ends)]),
                cells,
                lax.ppermute(head, axis, [((i + 1) % count, i) for i in range(ends)]),
            ],
            axis=dim,
        )
    return cells


def on_device(
    initial_temp,
    land_mask,
    pert_table,
    pert_index,
    base_kh,
    member_mix,
    base_mix,
    owner,
    column,
    interp_w,
    obs_inv_var,
    observed,
):
    members = pert_index.shape[0]
    levels = initial_temp.shape[0]
    width_lon = initial_temp.shape[1]
    width_lat = initial_temp.shape[2]
    table_rows = pert_table.shape[0]
    chooser = (pert_index[:, None] == jnp.arange(table_rows)[None, :]).astype(jnp.float32)
    member_kh = jnp.dot(chooser, pert_table, precision=lax.Precision.HIGHEST)
    run_kh = jnp.concatenate([member_kh, base_kh[None, :]], 0)
    run_mix = jnp.concatenate([member_mix, base_mix[None]], 0)
    run_count = members + 1
    fields = jnp.broadcast_to(
        initial_temp.astype(jnp.bfloat16)[None], (run_count, levels, width_lon, width_lat)
    )
    total_lat = width_lat * lax.axis_size("lat")
    lat_start = lax.axis_index("lat") * width_lat
    ocean_open = land_mask.astype(jnp.float32)
    for step_index in range(STEPS):
        lon_padded = padded_2(fields, (("lon", 2),), 1, True)
        padded = padded_2(lon_padded, (("lat", 3),), 1, False)
        global_rows = lat_start - (1 - 1) + jnp.arange(width_lat + 2 * (1 - 1))
        has_next = (global_rows < total_lat - 1).astype(jnp.float32)
        has_prior = (global_rows > 0).astype(jnp.float32)
        widened = padded.astype(jnp.float32)
        values = widened[:, :, 1:-1, 1:-1]
        laplace = widened[:, :, 2:, 1:-1] + widened[:, :, :-2, 1:-1] - 2.0 * values
        laplace = (
            laplace
            + has_next * (widened[:, :, 1:-1, 2:] - values)
            + has_prior * (widened[:, :, 1:-1, :-2] - values)
        )
        right_side = (values + run_kh[:, :, None, None] * laplace).astype(jnp.bfloat16)
        vertical = right_side.astype(jnp.float32) + jnp.einsum(
            "rkj,rjab->rkab", run_mix, right_side, preferred_element_type=jnp.float32
        )
        fields = (values + ocean_open * (vertical - values)).astype(jnp.bfloat16)
    owners = lax.axis_size("lat") * lax.axis_size("lon")
    prof_dev = owner.shape[0]
    capacity = max(2, 2 * prof_dev // owners)
    target = owner[:, 0]
    matches = (target[:, None] == jnp.arange(owners)[None, :]).astype(jnp.int32)
    earlier = jnp.cumsum(matches, 0) - matches
    slot_rank = jnp.sum(earlier * matches, 1)
    position = target * capacity + slot_rank
    send_ids = (
        jnp.full((owners * capacity,), -1, jnp.int32)
        .at[position]
        .set(column)
        .reshape(owners, capacity)
    )
    records = jnp.stack([interp_w, obs_inv_var, observed], 1)
    send_records = (
        jnp.zeros((owners * capacity, 3, levels), jnp.float32)
        .at[position]
        .set(records)
        .reshape(owners, capacity, 3, levels)
    )
    columns_flat = fields.reshape(run_count, levels, width_lon * width_lat)
    column_ids = lax.all_to_all(send_ids, ("lat", "lon"), split_axis=0, concat_axis=0, tiled=True)
    record_rows = lax.all_to_all(
        send_records, ("lat", "lon"), split_axis=0, concat_axis=0, tiled=True
    )
    sources = column_ids.shape[0]
    slot_count = column_ids.shape[1]
    usable = (column_ids >= 0).astype(jnp.float32).reshape(-1)
    picked = jnp.take(columns_flat, jnp.maximum(column_ids, 0).reshape(-1), axis=2).astype(
        jnp.float32
    )
    deeper = jnp.concatenate([picked[:, 1:], picked[:, -1:]], 1)
    flat_records = record_rows.reshape(sources * slot_count, 3, levels)
    weight = flat_records[:, 0].T
    inv_var = flat_records[:, 1].T * usable
    measured = flat_records[:, 2].T
    modeled = weight * picked + (1.0 - weight) * deeper
    green_cols = ((modeled[:members] - modeled[members]) * usable).astype(jnp.bfloat16)
    misfit = (measured - modeled[members]) * usable
    extras = jnp.stack([inv_var, misfit], 0)
    green_cols, extras = (
        green_cols.reshape(members, levels, sources, slot_count),
        extras.reshape(2, levels, sources, slot_count),
    )
    owner_misfit = jnp.transpose(extras[1], (1, 2, 0))
    returned = lax.all_to_all(owner_misfit, ("lat", "lon"), split_axis=0, concat_axis=0, tiled=True)
    misfit_rows = jnp.take(returned.reshape(owners * capacity, levels), position, axis=0)
    green_cols = green_cols.reshape(members, levels, -1)
    extras = extras.reshape(2, levels, -1)
    normalizer = 1.0 / (prof_dev * owners * levels)
    green_all = lax.all_gather(green_cols, "mem", axis=0, tiled=True)
    green_float = green_all.astype(jnp.float32)
    weighted = green_float * extras[0]
    gram_part = (
        jnp.einsum("mks,nks->mn", weighted, green_float, precision=lax.Precision.HIGHEST)
        * normalizer
    )
    proj_part = (
        jnp.einsum("mks,ks->m", weighted, extras[1], precision=lax.Precision.HIGHEST) * normalizer
    )
    gram_part, proj_part = (gram_part, proj_part)
    gram_block, projection = lax.psum((gram_part, proj_part), ("lat", "lon"))
    return (fields[:members], fields[members], gram_block, projection, misfit_rows)


def solution(mesh):
    placed = (
        P(None, "lon", "lat"),
        P("lon", "lat"),
        P(),
        P("mem"),
        P(),
        P("mem", None, None),
        P(),
        P(("lat", "lon"), None),
        P(("lat", "lon")),
        P(("lat", "lon"), None),
        P(("lat", "lon"), None),
        P(("lat", "lon"), None),
    )
    return jax.shard_map(
        on_device,
        mesh=mesh,
        in_specs=placed,
        out_specs=(
            P("mem", None, "lon", "lat"),
            P(None, "lon", "lat"),
            P(),
            P(),
            P(("lat", "lon"), None),
        ),
        check_vma=False,
    )
```

profile of v0, /device:TPU:258, one launch (start us, length us, event | category | flops | bytes accessed | tf_op | source)
XLA Modules:
  0.0 559.3 jit_solution(4841442048766482967)
XLA Ops:
  1.6 4.6 collective-permute-start.1
  6.3 1.9 collective-permute-start
  10.8 5.7 %collective-permute-done = bf16[3,100,1,128]{3,1,2,0:T(8,128)(2,1)S(1)} collective-permute-done((bf16[3,100,1,128]{3,1,2,0:T(8,128)(2,1)S(1)}, bf16[3,100,1,128]{3,1,2,0:T(8,128)(2,1)S(1)}, u32[]{:S(2)}, u32[]{:S(2)}) %collective-permute-start) | collective-permute-done | bytes 76832 | tf_op jit(solution)/shard_map/ppermute | solution.py:17
  19.6 5.7 %collective-permute-done.3 = bf16[3,100,6,1]{3,1,2,0:T(8,128)(2,1)S(1)} collective-permute-done((bf16[3,100,6,1]{3,1,2,0:T(8,128)(2,1)S(1)}, bf16[3,100,6,1]{3,1,2,0:T(8,128)(2,1)S(1)}, u32[]{:S(2)}, u32[]{:S(2)}) %collective-permute-start.3) | collective-permute-done | bytes 3632 | tf_op jit(solution)/shard_map/ppermute | solution.py:19
  27.4 1.9 collective-permute-start.4
  29.4 7.8 %collective-permute-start.5 = (bf16[3,100,1,128]{3,1,2,0:T(8,128)(2,1)S(1)}, bf16[3,100,1,128]{3,1,2,0:T(8,128)(2,1)S(1)}, u32[]{:S(2)}, u32[]{:S(2)}) collective-permute-start(bf16[3,100,1,128]{3,1,2,0:T(8,128)(2,1)S(1)} %get-tuple-element.41), channel_id=1, source_target_pairs={{1,0},{2,1},{3,2},{4,3},{5,4},{6,5},{7,6},{8,7},{9,8},{10,9},{11,1... | collective-permute-start | bytes 230408 | tf_op jit(solution)/shard_map/ppermute | solution.py:19
  39.5 13.3 %collective-permute-start.6 = (bf16[3,100,6,1]{3,1,2,0:T(8,128)(2,1)S(1)}, bf16[3,100,6,1]{3,1,2,0:T(8,128)(2,1)S(1)}, u32[]{:S(2)}, u32[]{:S(2)}) collective-permute-start(bf16[3,100,6,1]{3,1,2,0:T(8,128)(2,1)S(1)} %get-tuple-element.30), channel_id=1, source_target_pairs={{0,32},{32,64},{64,96},{1,33},{33,65},{65,97},{2,34},{34,66},{66,9... | collective-permute-start | bytes 10808 | tf_op jit(solution)/shard_map/ppermute | solution.py:17
  56.4 18.1 %all-to-all-start.1 = ((s32[128,1,4]{2,1,0:T(1,128)}), s32[128,1,4]{2,1,0:T(1,128)S(1)}, u32[]{:S(2)}, u32[]{:S(2)}) async-start(s32[128,1,4]{2,1,0:T(1,128)} %bitcast.22), calls=%async_computation.1 | async-start | bytes 131072 | tf_op jit(solution)/shard_map/all_to_all | solution.py:97
  75.2 1.6 fusion.20
  76.8 3.4 collective-permute-start.8
  80.2 6.4 %collective-permute-start.9 = (bf16[3,100,1,128]{3,1,2,0:T(8,128)(2,1)S(1)}, bf16[3,100,1,128]{3,1,2,0:T(8,128)(2,1)S(1)}, u32[]{:S(2)}, u32[]{:S(2)}) collective-permute-start(bf16[3,100,1,128]{3,1,2,0:T(8,128)(2,1)S(1)} %get-tuple-element.39), channel_id=1, source_target_pairs={{1,0},{2,1},{3,2},{4,3},{5,4},{6,5},{7,6},{8,7},{9,8},{10,9},{11,1... | collective-permute-start | bytes 230408 | tf_op jit(solution)/shard_map/ppermute | solution.py:19
  93.0 7.1 %scatter_fusion = f32[512,3,100]{2,1,0:T(4,128)S(1)} fusion(f32[512,3,100]{2,1,0:T(4,128)S(1)} %broadcast_in_dim.33, s32[256]{0:T(256)S(1)} %bitcast.104, f32[256,3,100]{2,1,0:T(4,128)S(1)} %copy.45), kind=kCustom, calls=%fused_computation.2 | custom fusion | bytes 922624 | tf_op jit(solution)/shard_map/scatter | solution.py:93
  103.3 1.9 collective-permute-start.12
  105.2 8.2 %collective-permute-start.13 = (bf16[3,100,1,128]{3,1,2,0:T(8,128)(2,1)S(1)}, bf16[3,100,1,128]{3,1,2,0:T(8,128)(2,1)S(1)}, u32[]{:S(2)}, u32[]{:S(2)}) collective-permute-start(bf16[3,100,1,128]{3,1,2,0:T(8,128)(2,1)S(1)} %get-tuple-element.37), channel_id=1, source_target_pairs={{1,0},{2,1},{3,2},{4,3},{5,4},{6,5},{7,6},{8,7},{9,8},{10,9},{11,1... | collective-permute-start | bytes 230408 | tf_op jit(solution)/shard_map/ppermute | solution.py:19
  113.4 21.5 %all-to-all-start = ((f32[128,4,3,100]{3,1,2,0:T(4,128)}), f32[128,4,3,100]{3,1,2,0:T(4,128)S(1)}, u32[]{:S(2)}, u32[]{:S(2)}) async-start(f32[128,4,3,100]{3,1,2,0:T(4,128)} %copy.47), calls=%async_computation | async-start | bytes 1572864 | tf_op jit(solution)/shard_map/all_to_all | solution.py:98
  135.5 2.3 collective-permute-start.14
  140.1 6.5 %collective-permute-done.15 = bf16[3,100,6,1]{3,1,2,0:T(8,128)(2,1)} collective-permute-done((bf16[3,100,6,1]{3,1,2,0:T(8,128)(2,1)S(1)}, bf16[3,100,6,1]{3,1,2,0:T(8,128)(2,1)}, u32[]{:S(2)}, u32[]{:S(2)}) %collective-permute-start.15) | collective-permute-done | bytes 3632 | tf_op jit(solution)/shard_map/ppermute | solution.py:19
  146.7 1.7 maximum_convert_fusion.3
  150.0 2.5 collective-permute-start.16
  152.5 7.3 %collective-permute-start.17 = (bf16[3,100,1,128]{3,1,2,0:T(8,128)(2,1)S(1)}, bf16[3,100,1,128]{3,1,2,0:T(8,128)(2,1)S(1)}, u32[]{:S(2)}, u32[]{:S(2)}) collective-permute-start(bf16[3,100,1,128]{3,1,2,0:T(8,128)(2,1)S(1)} %get-tuple-element.35), channel_id=1, source_target_pairs={{1,0},{2,1},{3,2},{4,3},{5,4},{6,5},{7,6},{8,7},{9,8},{10,9},{11,1... | collective-permute-start | bytes 230408 | tf_op jit(solution)/shard_map/ppermute | solution.py:19
  160.0 1.6 collective-permute-done.16
  162.1 23.8 %collective-permute-start.18 = (bf16[3,100,6,1]{3,1,2,0:T(8,128)(2,1)S(1)}, bf16[3,100,6,1]{3,1,2,0:T(8,128)(2,1)S(1)}, u32[]{:S(2)}, u32[]{:S(2)}) collective-permute-start(bf16[3,100,6,1]{3,1,2,0:T(8,128)(2,1)S(1)} %get-tuple-element.24), channel_id=1, source_target_pairs={{0,32},{32,64},{64,96},{1,33},{33,65},{65,97},{2,34},{34,66},{66,9... | collective-permute-start | bytes 10808 | tf_op jit(solution)/shard_map/ppermute | solution.py:17
  188.5 1.7 collective-permute-done.19
  190.2 1.7 maximum_convert_fusion.4
  194.3 2.1 gather_fusion
  196.4 1.8 convert_bitcast_fusion
  201.2 1.9 fusion.36
  206.1 24.3 %all-to-all-start.2 = ((f32[128,4,100]{2,1,0:T(4,128)}), f32[128,4,100]{2,1,0:T(4,128)S(1)}, u32[]{:S(2)}, u32[]{:S(2)}) async-start(f32[128,4,100]{2,1,0:T(4,128)} %bitcast.35), calls=%async_computation.2 | async-start | bytes 524288 | tf_op jit(solution)/shard_map/all_to_all | solution.py:121
  231.5 14.8 %all_gather.3 = bf16[8,100,512]{2,1,0:T(8,128)(2,1)S(1)} all-gather(bf16[2,100,512]{2,1,0:T(8,128)(2,1)S(1)} %copy.52), channel_id=1, replica_groups=mesh['mem'=4,'lat'=4,'lon'=32] {'mem'}, dimensions={0}, use_global_device_ids=true | all-gather | bytes 1024000 | tf_op jit(solution)/shard_map/all_gather | solution.py:126
  246.6 3.9 fusion.33
  250.4 2.6 fusion.27
  253.0 304.7 %all-reduce = (f32[8,8]{1,0:T(8,128)}, f32[8]{0:T(128)}) all-reduce(f32[8,8]{1,0:T(8,128)S(1)} %fusion.27, f32[8]{0:T(128)S(1)} %fusion.33), channel_id=1, replica_groups=mesh['mem'=4,'lat'=4,'lon'=32] {'lat','lon'}, use_global_device_ids=true, to_apply=%region_5.6 | all-reduce | flops 72 | bytes 576 | tf_op jit(solution)/shard_map/psum | solution.py:137
  (126 shorter events, 43.7 us)
Async XLA Ops:
  0.6 8.6 %copy-start = (f32[16,100]{1,0:T(8,128)S(1)}, f32[16,100]{1,0:T(8,128)}, u32[]{:S(2)}) copy-start(f32[16,100]{1,0:T(8,128)} %param.14) | copy-start | bytes 19204
  1.6 9.2 %collective-permute-start.1 = (bf16[3,100,1,128]{3,1,2,0:T(8,128)(2,1)S(1)}, bf16[3,100,1,128]{3,1,2,0:T(8,128)(2,1)S(1)}, u32[]{:S(2)}, u32[]{:S(2)}) collective-permute-start(bf16[3,100,1,128]{3,1,2,0:T(8,128)(2,1)S(1)} %broadcast_in_dim.30), channel_id=1, source_target_pairs={{1,0},{2,1},{3,2},{4,3},{5,4},{6,5},{7,6},{8,7},{9,8},{10,9},{11,1... | collective-permute-start | bytes 230408 | tf_op jit(solution)/shard_map/ppermute | solution.py:19
  6.3 10.2 %collective-permute-start = (bf16[3,100,1,128]{3,1,2,0:T(8,128)(2,1)S(1)}, bf16[3,100,1,128]{3,1,2,0:T(8,128)(2,1)S(1)}, u32[]{:S(2)}, u32[]{:S(2)}) collective-permute-start(bf16[3,100,1,128]{3,1,2,0:T(8,128)(2,1)S(1)} %broadcast_in_dim.28), channel_id=1, source_target_pairs={{0,1},{1,2},{2,3},{3,4},{4,5},{5,6},{6,7},{7,8},{8,9},{9,10},{10,1... | collective-permute-start | bytes 230408 | tf_op jit(solution)/shard_map/ppermute | solution.py:17
  9.0 10.5 %copy-start.10 = (s32[4,128]{1,0:T(4,128)S(1)}, s32[4,128]{1,0:T(4,128)}, u32[]{:S(2)}) copy-start(s32[4,128]{1,0:T(4,128)} %param.13) | copy-start | bytes 6148
  9.0 10.5 %copy-start.8 = (bf16[2,100,100]{2,0,1:T(2,128)(2,1)S(1)}, bf16[2,100,100]{2,0,1:T(2,128)(2,1)}, u32[]{:S(2)}) copy-start(bf16[2,100,100]{2,0,1:T(2,128)(2,1)} %param.17) | copy-start | bytes 120004
  16.8 9.0 %copy-start.11 = (bf16[100,100]{1,0:T(8,128)(2,1)S(1)}, bf16[100,100]{1,0:T(8,128)(2,1)}, u32[]{:S(2)}) copy-start(bf16[100,100]{1,0:T(8,128)(2,1)} %param.18) | copy-start | bytes 60004
  16.8 2.8 collective-permute-start.2
  18.1 7.1 %collective-permute-start.3 = (bf16[3,100,6,1]{3,1,2,0:T(8,128)(2,1)S(1)}, bf16[3,100,6,1]{3,1,2,0:T(8,128)(2,1)S(1)}, u32[]{:S(2)}, u32[]{:S(2)}) collective-permute-start(bf16[3,100,6,1]{3,1,2,0:T(8,128)(2,1)S(1)} %get-tuple-element.33), channel_id=1, source_target_pairs={{32,0},{64,32},{96,64},{33,1},{65,33},{97,65},{34,2},{66,34},{98,6... | collective-permute-start | bytes 10808 | tf_op jit(solution)/shard_map/ppermute | solution.py:19
  25.8 11.4 %copy-start.9 = (s32[256,1]{0,1:T(1,128)S(1)}, s32[256,1]{0,1:T(1,128)}, u32[]{:S(2)}) copy-start(s32[256,1]{0,1:T(1,128)} %param.19) | copy-start | bytes 3076
  27.4 10.2 %collective-permute-start.4 = (bf16[3,100,1,128]{3,1,2,0:T(8,128)(2,1)S(1)}, bf16[3,100,1,128]{3,1,2,0:T(8,128)(2,1)S(1)}, u32[]{:S(2)}, u32[]{:S(2)}) collective-permute-start(bf16[3,100,1,128]{3,1,2,0:T(8,128)(2,1)S(1)} %get-tuple-element.40), channel_id=1, source_target_pairs={{0,1},{1,2},{2,3},{3,4},{4,5},{5,6},{6,7},{7,8},{8,9},{9,10},{10,1... | collective-permute-start | bytes 230408 | tf_op jit(solution)/shard_map/ppermute | solution.py:17
  29.4 9.9 %collective-permute-start.5 = (bf16[3,100,1,128]{3,1,2,0:T(8,128)(2,1)S(1)}, bf16[3,100,1,128]{3,1,2,0:T(8,128)(2,1)S(1)}, u32[]{:S(2)}, u32[]{:S(2)}) collective-permute-start(bf16[3,100,1,128]{3,1,2,0:T(8,128)(2,1)S(1)} %get-tuple-element.41), channel_id=1, source_target_pairs={{1,0},{2,1},{3,2},{4,3},{5,4},{6,5},{7,6},{8,7},{9,8},{10,9},{11,1... | collective-permute-start | bytes 230408 | tf_op jit(solution)/shard_map/ppermute | solution.py:19
  39.5 35.1 %collective-permute-start.6 = (bf16[3,100,6,1]{3,1,2,0:T(8,128)(2,1)S(1)}, bf16[3,100,6,1]{3,1,2,0:T(8,128)(2,1)S(1)}, u32[]{:S(2)}, u32[]{:S(2)}) collective-permute-start(bf16[3,100,6,1]{3,1,2,0:T(8,128)(2,1)S(1)} %get-tuple-element.30), channel_id=1, source_target_pairs={{0,32},{32,64},{64,96},{1,33},{33,65},{65,97},{2,34},{34,66},{66,9... | collective-permute-start | bytes 10808 | tf_op jit(solution)/shard_map/ppermute | solution.py:17
  52.8 21.8 %collective-permute-start.7 = (bf16[3,100,6,1]{3,1,2,0:T(8,128)(2,1)S(1)}, bf16[3,100,6,1]{3,1,2,0:T(8,128)(2,1)S(1)}, u32[]{:S(2)}, u32[]{:S(2)}) collective-permute-start(bf16[3,100,6,1]{3,1,2,0:T(8,128)(2,1)S(1)} %get-tuple-element.31), channel_id=1, source_target_pairs={{32,0},{64,32},{96,64},{33,1},{65,33},{97,65},{34,2},{66,34},{98,6... | collective-permute-start | bytes 10808 | tf_op jit(solution)/shard_map/ppermute | solution.py:19
  56.4 57.0 %all-to-all-start.1 = ((s32[128,1,4]{2,1,0:T(1,128)}), s32[128,1,4]{2,1,0:T(1,128)S(1)}, u32[]{:S(2)}, u32[]{:S(2)}) async-start(s32[128,1,4]{2,1,0:T(1,128)} %bitcast.22), calls=%async_computation.1 | async-start | bytes 131072 | tf_op jit(solution)/shard_map/all_to_all | solution.py:97
  75.1 11.4 %copy-start.5 = (f32[256,100]{0,1:T(8,128)S(1)}, f32[256,100]{0,1:T(8,128)}, u32[]{:S(2)}) copy-start(f32[256,100]{0,1:T(8,128)} %param.23) | copy-start | bytes 307204
  75.1 11.4 %copy-start.6 = (f32[256,100]{0,1:T(8,128)S(1)}, f32[256,100]{0,1:T(8,128)}, u32[]{:S(2)}) copy-start(f32[256,100]{0,1:T(8,128)} %param.22) | copy-start | bytes 307204
  75.1 11.4 %copy-start.7 = (f32[256,100]{0,1:T(8,128)S(1)}, f32[256,100]{0,1:T(8,128)}, u32[]{:S(2)}) copy-start(f32[256,100]{0,1:T(8,128)} %param.21) | copy-start | bytes 307204
  76.8 10.5 %collective-permute-start.8 = (bf16[3,100,1,128]{3,1,2,0:T(8,128)(2,1)S(1)}, bf16[3,100,1,128]{3,1,2,0:T(8,128)(2,1)S(1)}, u32[]{:S(2)}, u32[]{:S(2)}) collective-permute-start(bf16[3,100,1,128]{3,1,2,0:T(8,128)(2,1)S(1)} %get-tuple-element.38), channel_id=1, source_target_pairs={{0,1},{1,2},{2,3},{3,4},{4,5},{5,6},{6,7},{7,8},{8,9},{9,10},{10,1... | collective-permute-start | bytes 230408 | tf_op jit(solution)/shard_map/ppermute | solution.py:17
  80.2 8.4 %collective-permute-start.9 = (bf16[3,100,1,128]{3,1,2,0:T(8,128)(2,1)S(1)}, bf16[3,100,1,128]{3,1,2,0:T(8,128)(2,1)S(1)}, u32[]{:S(2)}, u32[]{:S(2)}) collective-permute-start(bf16[3,100,1,128]{3,1,2,0:T(8,128)(2,1)S(1)} %get-tuple-element.39), channel_id=1, source_target_pairs={{1,0},{2,1},{3,2},{4,3},{5,4},{6,5},{7,6},{8,7},{9,8},{10,9},{11,1... | collective-permute-start | bytes 230408 | tf_op jit(solution)/shard_map/ppermute | solution.py:19
  89.8 11.4 %collective-permute-start.10 = (bf16[3,100,6,1]{3,1,2,0:T(8,128)(2,1)}, bf16[3,100,6,1]{3,1,2,0:T(8,128)(2,1)S(1)}, u32[]{:S(2)}, u32[]{:S(2)}) collective-permute-start(bf16[3,100,6,1]{3,1,2,0:T(8,128)(2,1)} %get-tuple-element.28), channel_id=1, source_target_pairs={{0,32},{32,64},{64,96},{1,33},{33,65},{65,97},{2,34},{34,66},{66,9... | collective-permute-start | bytes 10808 | tf_op jit(solution)/shard_map/ppermute | solution.py:17
  91.1 10.1 %collective-permute-start.11 = (bf16[3,100,6,1]{3,1,2,0:T(8,128)(2,1)}, bf16[3,100,6,1]{3,1,2,0:T(8,128)(2,1)S(1)}, u32[]{:S(2)}, u32[]{:S(2)}) collective-permute-start(bf16[3,100,6,1]{3,1,2,0:T(8,128)(2,1)} %get-tuple-element.29), channel_id=1, source_target_pairs={{32,0},{64,32},{96,64},{33,1},{65,33},{97,65},{34,2},{66,34},{98,6... | collective-permute-start | bytes 10808 | tf_op jit(solution)/shard_map/ppermute | solution.py:19
  103.3 31.9 %collective-permute-start.12 = (bf16[3,100,1,128]{3,1,2,0:T(8,128)(2,1)S(1)}, bf16[3,100,1,128]{3,1,2,0:T(8,128)(2,1)S(1)}, u32[]{:S(2)}, u32[]{:S(2)}) collective-permute-start(bf16[3,100,1,128]{3,1,2,0:T(8,128)(2,1)S(1)} %get-tuple-element.36), channel_id=1, source_target_pairs={{0,1},{1,2},{2,3},{3,4},{4,5},{5,6},{6,7},{7,8},{8,9},{9,10},{10,1... | collective-permute-start | bytes 230408 | tf_op jit(solution)/shard_map/ppermute | solution.py:17
  105.2 30.0 %collective-permute-start.13 = (bf16[3,100,1,128]{3,1,2,0:T(8,128)(2,1)S(1)}, bf16[3,100,1,128]{3,1,2,0:T(8,128)(2,1)S(1)}, u32[]{:S(2)}, u32[]{:S(2)}) collective-permute-start(bf16[3,100,1,128]{3,1,2,0:T(8,128)(2,1)S(1)} %get-tuple-element.37), channel_id=1, source_target_pairs={{1,0},{2,1},{3,2},{4,3},{5,4},{6,5},{7,6},{8,7},{9,8},{10,9},{11,1... | collective-permute-start | bytes 230408 | tf_op jit(solution)/shard_map/ppermute | solution.py:19
  113.4 87.4 %all-to-all-start = ((f32[128,4,3,100]{3,1,2,0:T(4,128)}), f32[128,4,3,100]{3,1,2,0:T(4,128)S(1)}, u32[]{:S(2)}, u32[]{:S(2)}) async-start(f32[128,4,3,100]{3,1,2,0:T(4,128)} %copy.47), calls=%async_computation | async-start | bytes 1572864 | tf_op jit(solution)/shard_map/all_to_all | solution.py:98
  135.5 3.9 collective-permute-start.14
  137.8 8.9 %collective-permute-start.15 = (bf16[3,100,6,1]{3,1,2,0:T(8,128)(2,1)S(1)}, bf16[3,100,6,1]{3,1,2,0:T(8,128)(2,1)}, u32[]{:S(2)}, u32[]{:S(2)}) collective-permute-start(bf16[3,100,6,1]{3,1,2,0:T(8,128)(2,1)S(1)} %get-tuple-element.27), channel_id=1, source_target_pairs={{32,0},{64,32},{96,64},{33,1},{65,33},{97,65},{34,2},{66,34},{98,6... | collective-permute-start | bytes 10808 | tf_op jit(solution)/shard_map/ppermute | solution.py:19
  150.0 11.6 %collective-permute-start.16 = (bf16[3,100,1,128]{3,1,2,0:T(8,128)(2,1)S(1)}, bf16[3,100,1,128]{3,1,2,0:T(8,128)(2,1)S(1)}, u32[]{:S(2)}, u32[]{:S(2)}) collective-permute-start(bf16[3,100,1,128]{3,1,2,0:T(8,128)(2,1)S(1)} %get-tuple-element.34), channel_id=1, source_target_pairs={{0,1},{1,2},{2,3},{3,4},{4,5},{5,6},{6,7},{7,8},{8,9},{9,10},{10,1... | collective-permute-start | bytes 230408 | tf_op jit(solution)/shard_map/ppermute | solution.py:17
  152.5 9.4 %collective-permute-start.17 = (bf16[3,100,1,128]{3,1,2,0:T(8,128)(2,1)S(1)}, bf16[3,100,1,128]{3,1,2,0:T(8,128)(2,1)S(1)}, u32[]{:S(2)}, u32[]{:S(2)}) collective-permute-start(bf16[3,100,1,128]{3,1,2,0:T(8,128)(2,1)S(1)} %get-tuple-element.35), channel_id=1, source_target_pairs={{1,0},{2,1},{3,2},{4,3},{5,4},{6,5},{7,6},{8,7},{9,8},{10,9},{11,1... | collective-permute-start | bytes 230408 | tf_op jit(solution)/shard_map/ppermute | solution.py:19
  162.1 25.6 %collective-permute-start.18 = (bf16[3,100,6,1]{3,1,2,0:T(8,128)(2,1)S(1)}, bf16[3,100,6,1]{3,1,2,0:T(8,128)(2,1)S(1)}, u32[]{:S(2)}, u32[]{:S(2)}) collective-permute-start(bf16[3,100,6,1]{3,1,2,0:T(8,128)(2,1)S(1)} %get-tuple-element.24), channel_id=1, source_target_pairs={{0,32},{32,64},{64,96},{1,33},{33,65},{65,97},{2,34},{34,66},{66,9... | collective-permute-start | bytes 10808 | tf_op jit(solution)/shard_map/ppermute | solution.py:17
  186.0 4.2 collective-permute-start.19
  198.1 1.9 slice-start
  206.1 351.7 %all-to-all-start.2 = ((f32[128,4,100]{2,1,0:T(4,128)}), f32[128,4,100]{2,1,0:T(4,128)S(1)}, u32[]{:S(2)}, u32[]{:S(2)}) async-start(f32[128,4,100]{2,1,0:T(4,128)} %bitcast.35), calls=%async_computation.2 | async-start | bytes 524288 | tf_op jit(solution)/shard_map/all_to_all | solution.py:121
  (4 other events, 3.5 us)
where the time goes:
time: 560 us; the launch traced here: 559 us
  blocking collectives  320 us (57%)
  starting transfers between devices  159 us (28%)
  local copies, waits for them, and re-layouts  25.4 us (5%)
  waiting for transfers between devices  25.4 us (5%)
  matrix products  15.2 us (3%)
  other arithmetic  13.8 us (2%)
    psum x1, blocking collectives, on_device(): gram_block, projection = lax.psum((gram_part, proj_part), ('lat', 'lon'))  305 us
    ppermute x10, starting transfers between devices, padded_2(): lax.ppermute(tail, axis, [(i, (i + 1) % count) for i in range(ends)])  53.6 us
    ppermute x10, starting transfers between devices, padded_2(): lax.ppermute(head, axis, [((i + 1) % count, i) for i in range(ends)])  41.1 us
    all_to_all x1, starting transfers between devices, on_device(): lax.all_to_all(owner_misfit, ('lat', 'lon'), split_axis=0, concat_axis=0,...  24.3 us
    all_to_all x1, starting transfers between devices, on_device(): lax.all_to_all(send_records, ('lat', 'lon'), split_axis=0, concat_axis=0,...  21.5 us
    all_to_all x1, starting transfers between devices, on_device(): lax.all_to_all(send_ids, ('lat', 'lon'), split_axis=0, concat_axis=0, til...  18.1 us
    ppermute x10, waiting for transfers between devices, padded_2(): lax.ppermute(head, axis, [((i + 1) % count, i) for i in range(ends)])  17.1 us
    all_gather x1, blocking collectives, on_device(): green_all = lax.all_gather(green_cols, 'mem', axis=0, tiled=True)  14.8 us
  transfers between devices with their start and end apart: 23, of which 10 were waited for; matrix products, arithmetic and copies ran while one was open for 7% of the time, Pallas kernels for 0%

commit v1 on v0

--- a/solution.py
+++ b/solution.py
@@ -134,7 +134,7 @@
         jnp.einsum("mks,ks->m", weighted, extras[1], precision=lax.Precision.HIGHEST) * normalizer
     )
     gram_part, proj_part = (gram_part, proj_part)
-    gram_block, projection = lax.psum((gram_part, proj_part), ("lat", "lon"))
+    gram_block, projection = lax.psum(lax.psum((gram_part, proj_part), "lon"), "lat")
     return (fields[:members], fields[members], gram_block, projection, misfit_rows)
 
 

time: 560 us -> 352 us (0.63)
  the two profiles are of different devices: /device:TPU:258 before, /device:TPU:1 now
where the time goes in v1:
time: 352 us; the launch traced here: 351 us
  starting transfers between devices  123 us (35%)
  blocking collectives  106 us (30%)
  waiting for transfers between devices  65.5 us (19%)
  local copies, waits for them, and re-layouts  25.4 us (7%)
  matrix products  15.2 us (4%)
  other arithmetic  13.8 us (4%)
    psum x1, blocking collectives, on_device(): lax.psum((gram_part, proj_part), 'lon')  68 us
    ppermute x10, starting transfers between devices, padded_2(): lax.ppermute(head, axis, [((i + 1) % count, i) for i in range(ends)])  51.4 us
    ppermute x10, starting transfers between devices, padded_2(): lax.ppermute(tail, axis, [(i, (i + 1) % count) for i in range(ends)])  40.7 us
    ppermute x10, waiting for transfers between devices, padded_2(): lax.ppermute(head, axis, [((i + 1) % count, i) for i in range(ends)])  40.1 us
    ppermute x10, waiting for transfers between devices, padded_2(): lax.ppermute(tail, axis, [(i, (i + 1) % count) for i in range(ends)])  25.4 us
    psum x1, blocking collectives, on_device(): lax.psum(lax.psum((gram_part, proj_part), 'lon'), 'lat')  25.4 us
    all_gather x1, blocking collectives, on_device(): green_all = lax.all_gather(green_cols, 'mem', axis=0, tiled=True)  12.9 us
    all_to_all x1, starting transfers between devices, on_device(): lax.all_to_all(send_ids, ('lat', 'lon'), split_axis=0, concat_axis=0, til...  12 us
  transfers between devices with their start and end apart: 23, of which 12 were waited for; matrix products, arithmetic and copies ran while one was open for 12% of the time, Pallas kernels for 0%

profile of v1, /device:TPU:1, one launch (start us, length us, event | category | flops | bytes accessed | tf_op | source)
XLA Modules:
  0.0 350.8 jit_solution(720471360907943509)
XLA Ops:
  1.6 14.5 %collective-permute-start.1 = (bf16[3,100,1,128]{3,1,2,0:T(8,128)(2,1)S(1)}, bf16[3,100,1,128]{3,1,2,0:T(8,128)(2,1)S(1)}, u32[]{:S(2)}, u32[]{:S(2)}) collective-permute-start(bf16[3,100,1,128]{3,1,2,0:T(8,128)(2,1)S(1)} %broadcast_in_dim.30), channel_id=1, source_target_pairs={{1,0},{2,1},{3,2},{4,3},{5,4},{6,5},{7,6},{8,7},{9,8},{10,9},{11,1... | collective-permute-start | bytes 230408 | tf_op jit(solution)/shard_map/ppermute | solution.py:19
  20.7 4.5 %collective-permute-done = bf16[3,100,1,128]{3,1,2,0:T(8,128)(2,1)S(1)} collective-permute-done((bf16[3,100,1,128]{3,1,2,0:T(8,128)(2,1)S(1)}, bf16[3,100,1,128]{3,1,2,0:T(8,128)(2,1)S(1)}, u32[]{:S(2)}, u32[]{:S(2)}) %collective-permute-start) | collective-permute-done | bytes 76832 | tf_op jit(solution)/shard_map/ppermute | solution.py:17
  25.6 6.7 %collective-permute-start.2 = (bf16[3,100,6,1]{3,1,2,0:T(8,128)(2,1)S(1)}, bf16[3,100,6,1]{3,1,2,0:T(8,128)(2,1)S(1)}, u32[]{:S(2)}, u32[]{:S(2)}) collective-permute-start(bf16[3,100,6,1]{3,1,2,0:T(8,128)(2,1)S(1)} %get-tuple-element.34), channel_id=1, source_target_pairs={{0,32},{32,64},{64,96},{1,33},{33,65},{65,97},{2,34},{34,66},{66,9... | collective-permute-start | bytes 10808 | tf_op jit(solution)/shard_map/ppermute | solution.py:17
  34.3 3.7 %collective-permute-done.2 = bf16[3,100,6,1]{3,1,2,0:T(8,128)(2,1)S(1)} collective-permute-done((bf16[3,100,6,1]{3,1,2,0:T(8,128)(2,1)S(1)}, bf16[3,100,6,1]{3,1,2,0:T(8,128)(2,1)S(1)}, u32[]{:S(2)}, u32[]{:S(2)}) %collective-permute-start.2) | collective-permute-done | bytes 3632 | tf_op jit(solution)/shard_map/ppermute | solution.py:17
  38.1 8.8 %collective-permute-done.3 = bf16[3,100,6,1]{3,1,2,0:T(8,128)(2,1)S(1)} collective-permute-done((bf16[3,100,6,1]{3,1,2,0:T(8,128)(2,1)S(1)}, bf16[3,100,6,1]{3,1,2,0:T(8,128)(2,1)S(1)}, u32[]{:S(2)}, u32[]{:S(2)}) %collective-permute-start.3) | collective-permute-done | bytes 3632 | tf_op jit(solution)/shard_map/ppermute | solution.py:19
  51.0 7.3 %collective-permute-start.5 = (bf16[3,100,1,128]{3,1,2,0:T(8,128)(2,1)S(1)}, bf16[3,100,1,128]{3,1,2,0:T(8,128)(2,1)S(1)}, u32[]{:S(2)}, u32[]{:S(2)}) collective-permute-start(bf16[3,100,1,128]{3,1,2,0:T(8,128)(2,1)S(1)} %get-tuple-element.43), channel_id=1, source_target_pairs={{1,0},{2,1},{3,2},{4,3},{5,4},{6,5},{7,6},{8,7},{9,8},{10,9},{11,1... | collective-permute-start | bytes 230408 | tf_op jit(solution)/shard_map/ppermute | solution.py:19
  60.0 2.9 collective-permute-start.6
  67.2 12.0 %all-to-all-start.1 = ((s32[128,1,4]{2,1,0:T(1,128)}), s32[128,1,4]{2,1,0:T(1,128)S(1)}, u32[]{:S(2)}, u32[]{:S(2)}) async-start(s32[128,1,4]{2,1,0:T(1,128)} %bitcast.22), calls=%async_computation.1 | async-start | bytes 131072 | tf_op jit(solution)/shard_map/all_to_all | solution.py:97
  81.4 3.3 collective-permute-start.8
  84.7 6.0 %collective-permute-start.9 = (bf16[3,100,1,128]{3,1,2,0:T(8,128)(2,1)S(1)}, bf16[3,100,1,128]{3,1,2,0:T(8,128)(2,1)S(1)}, u32[]{:S(2)}, u32[]{:S(2)}) collective-permute-start(bf16[3,100,1,128]{3,1,2,0:T(8,128)(2,1)S(1)} %get-tuple-element.41), channel_id=1, source_target_pairs={{1,0},{2,1},{3,2},{4,3},{5,4},{6,5},{7,6},{8,7},{9,8},{10,9},{11,1... | collective-permute-start | bytes 230408 | tf_op jit(solution)/shard_map/ppermute | solution.py:19
  93.5 8.6 %collective-permute-start.10 = (bf16[3,100,6,1]{3,1,2,0:T(8,128)(2,1)}, bf16[3,100,6,1]{3,1,2,0:T(8,128)(2,1)S(1)}, u32[]{:S(2)}, u32[]{:S(2)}) collective-permute-start(bf16[3,100,6,1]{3,1,2,0:T(8,128)(2,1)} %get-tuple-element.30), channel_id=1, source_target_pairs={{0,32},{32,64},{64,96},{1,33},{33,65},{65,97},{2,34},{34,66},{66,9... | collective-permute-start | bytes 10808 | tf_op jit(solution)/shard_map/ppermute | solution.py:17
  102.1 2.1 collective-permute-start.11
  104.6 7.1 %scatter_fusion = f32[512,3,100]{2,1,0:T(4,128)S(1)} fusion(f32[512,3,100]{2,1,0:T(4,128)S(1)} %broadcast_in_dim.33, s32[256]{0:T(256)S(1)} %bitcast.104, f32[256,3,100]{2,1,0:T(4,128)S(1)} %copy.45), kind=kCustom, calls=%fused_computation.2 | custom fusion | bytes 922624 | tf_op jit(solution)/shard_map/scatter | solution.py:93
  112.8 7.0 %collective-permute-done.11 = bf16[3,100,6,1]{3,1,2,0:T(8,128)(2,1)S(1)} collective-permute-done((bf16[3,100,6,1]{3,1,2,0:T(8,128)(2,1)}, bf16[3,100,6,1]{3,1,2,0:T(8,128)(2,1)S(1)}, u32[]{:S(2)}, u32[]{:S(2)}) %collective-permute-start.11) | collective-permute-done | bytes 3632 | tf_op jit(solution)/shard_map/ppermute | solution.py:19
  122.0 2.4 collective-permute-start.12
  124.5 6.7 %collective-permute-start.13 = (bf16[3,100,1,128]{3,1,2,0:T(8,128)(2,1)S(1)}, bf16[3,100,1,128]{3,1,2,0:T(8,128)(2,1)S(1)}, u32[]{:S(2)}, u32[]{:S(2)}) collective-permute-start(bf16[3,100,1,128]{3,1,2,0:T(8,128)(2,1)S(1)} %get-tuple-element.39), channel_id=1, source_target_pairs={{1,0},{2,1},{3,2},{4,3},{5,4},{6,5},{7,6},{8,7},{9,8},{10,9},{11,1... | collective-permute-start | bytes 230408 | tf_op jit(solution)/shard_map/ppermute | solution.py:19
  131.2 8.4 %all-to-all-start = ((f32[128,4,3,100]{3,1,2,0:T(4,128)}), f32[128,4,3,100]{3,1,2,0:T(4,128)S(1)}, u32[]{:S(2)}, u32[]{:S(2)}) async-start(f32[128,4,3,100]{3,1,2,0:T(4,128)} %copy.47), calls=%async_computation | async-start | bytes 1572864 | tf_op jit(solution)/shard_map/all_to_all | solution.py:98
  140.2 7.7 %collective-permute-start.14 = (bf16[3,100,6,1]{3,1,2,0:T(8,128)(2,1)S(1)}, bf16[3,100,6,1]{3,1,2,0:T(8,128)(2,1)S(1)}, u32[]{:S(2)}, u32[]{:S(2)}) collective-permute-start(bf16[3,100,6,1]{3,1,2,0:T(8,128)(2,1)S(1)} %get-tuple-element.28), channel_id=1, source_target_pairs={{0,32},{32,64},{64,96},{1,33},{33,65},{65,97},{2,34},{34,66},{66,9... | collective-permute-start | bytes 10808 | tf_op jit(solution)/shard_map/ppermute | solution.py:17
  150.1 13.9 %collective-permute-done.14 = bf16[3,100,6,1]{3,1,2,0:T(8,128)(2,1)S(1)} collective-permute-done((bf16[3,100,6,1]{3,1,2,0:T(8,128)(2,1)S(1)}, bf16[3,100,6,1]{3,1,2,0:T(8,128)(2,1)S(1)}, u32[]{:S(2)}, u32[]{:S(2)}) %collective-permute-start.14) | collective-permute-done | bytes 3632 | tf_op jit(solution)/shard_map/ppermute | solution.py:17
  164.7 9.6 %collective-permute-done.15 = bf16[3,100,6,1]{3,1,2,0:T(8,128)(2,1)} collective-permute-done((bf16[3,100,6,1]{3,1,2,0:T(8,128)(2,1)S(1)}, bf16[3,100,6,1]{3,1,2,0:T(8,128)(2,1)}, u32[]{:S(2)}, u32[]{:S(2)}) %collective-permute-start.15) | collective-permute-done | bytes 3632 | tf_op jit(solution)/shard_map/ppermute | solution.py:19
  177.7 2.4 collective-permute-start.16
  180.1 6.8 %collective-permute-start.17 = (bf16[3,100,1,128]{3,1,2,0:T(8,128)(2,1)S(1)}, bf16[3,100,1,128]{3,1,2,0:T(8,128)(2,1)S(1)}, u32[]{:S(2)}, u32[]{:S(2)}) collective-permute-start(bf16[3,100,1,128]{3,1,2,0:T(8,128)(2,1)S(1)} %get-tuple-element.37), channel_id=1, source_target_pairs={{1,0},{2,1},{3,2},{4,3},{5,4},{6,5},{7,6},{8,7},{9,8},{10,9},{11,1... | collective-permute-start | bytes 230408 | tf_op jit(solution)/shard_map/ppermute | solution.py:19
  188.6 2.8 collective-permute-start.18
  191.4 2.1 collective-permute-start.19
  193.8 3.2 collective-permute-done.18
  197.8 10.7 %collective-permute-done.19 = bf16[3,100,6,1]{3,1,2,0:T(8,128)(2,1)} collective-permute-done((bf16[3,100,6,1]{3,1,2,0:T(8,128)(2,1)S(1)}, bf16[3,100,6,1]{3,1,2,0:T(8,128)(2,1)}, u32[]{:S(2)}, u32[]{:S(2)}) %collective-permute-start.19) | collective-permute-done | bytes 3632 | tf_op jit(solution)/shard_map/ppermute | solution.py:19
  224.4 10.7 %all-to-all-start.2 = ((f32[128,4,100]{2,1,0:T(4,128)}), f32[128,4,100]{2,1,0:T(4,128)S(1)}, u32[]{:S(2)}, u32[]{:S(2)}) async-start(f32[128,4,100]{2,1,0:T(4,128)} %bitcast.35), calls=%async_computation.2 | async-start | bytes 524288 | tf_op jit(solution)/shard_map/all_to_all | solution.py:121
  236.2 12.9 %all_gather.3 = bf16[8,100,512]{2,1,0:T(8,128)(2,1)S(1)} all-gather(bf16[2,100,512]{2,1,0:T(8,128)(2,1)S(1)} %copy.52), channel_id=1, replica_groups=mesh['mem'=4,'lat'=4,'lon'=32] {'mem'}, dimensions={0}, use_global_device_ids=true | all-gather | bytes 1024000 | tf_op jit(solution)/shard_map/all_gather | solution.py:126
  249.4 3.9 %fusion.33 = f32[8]{0:T(128)S(1)} fusion(f32[100,512,1]{1,2,0:T(1,128)S(1)} %copy.60, f32[8,100,512]{2,1,0:T(8,128)S(1)} %convert_multiply_fusion), kind=kOutput, calls=%fused_computation.37 | convolution fusion | flops 4915208 | bytes 1843232 | tf_op jit(solution)/shard_map/mks,ks->m/dot_general | solution.py:134
  253.2 2.6 fusion.27
  255.8 68.0 %all-reduce = (f32[8,8]{1,0:T(8,128)S(1)}, f32[8]{0:T(128)S(1)}) all-reduce(f32[8,8]{1,0:T(8,128)S(1)} %fusion.27, f32[8]{0:T(128)S(1)} %fusion.33), channel_id=1, replica_groups=mesh['mem'=4,'lat'=4,'lon'=32] {'lon'}, use_global_device_ids=true, to_apply=%region_5.6 | all-reduce | flops 72 | bytes 576 | tf_op jit(solution)/shard_map/psum | solution.py:137
  323.8 25.4 %all-reduce.1 = (f32[8,8]{1,0:T(8,128)}, f32[8]{0:T(128)}) all-reduce(f32[8,8]{1,0:T(8,128)S(1)} %get-tuple-element.20, f32[8]{0:T(128)S(1)} %get-tuple-element.21), channel_id=1, replica_groups=mesh['mem'=4,'lat'=4,'lon'=32] {'lat'}, use_global_device_ids=true, to_apply=%region_6.7 | all-reduce | flops 72 | bytes 576 | tf_op jit(solution)/shard_map/psum | solution.py:137
  (127 shorter events, 54.4 us)
Async XLA Ops:
  0.6 18.6 %copy-start = (f32[16,100]{1,0:T(8,128)S(1)}, f32[16,100]{1,0:T(8,128)}, u32[]{:S(2)}) copy-start(f32[16,100]{1,0:T(8,128)} %param.14) | copy-start | bytes 19204
  1.6 19.1 %collective-permute-start.1 = (bf16[3,100,1,128]{3,1,2,0:T(8,128)(2,1)S(1)}, bf16[3,100,1,128]{3,1,2,0:T(8,128)(2,1)S(1)}, u32[]{:S(2)}, u32[]{:S(2)}) collective-permute-start(bf16[3,100,1,128]{3,1,2,0:T(8,128)(2,1)S(1)} %broadcast_in_dim.30), channel_id=1, source_target_pairs={{1,0},{2,1},{3,2},{4,3},{5,4},{6,5},{7,6},{8,7},{9,8},{10,9},{11,1... | collective-permute-start | bytes 230408 | tf_op jit(solution)/shard_map/ppermute | solution.py:19
  16.2 9.1 %collective-permute-start = (bf16[3,100,1,128]{3,1,2,0:T(8,128)(2,1)S(1)}, bf16[3,100,1,128]{3,1,2,0:T(8,128)(2,1)S(1)}, u32[]{:S(2)}, u32[]{:S(2)}) collective-permute-start(bf16[3,100,1,128]{3,1,2,0:T(8,128)(2,1)S(1)} %broadcast_in_dim.28), channel_id=1, source_target_pairs={{0,1},{1,2},{2,3},{3,4},{4,5},{5,6},{6,7},{7,8},{8,9},{9,10},{10,1... | collective-permute-start | bytes 230408 | tf_op jit(solution)/shard_map/ppermute | solution.py:17
  18.9 15.4 %copy-start.10 = (s32[4,128]{1,0:T(4,128)S(1)}, s32[4,128]{1,0:T(4,128)}, u32[]{:S(2)}) copy-start(s32[4,128]{1,0:T(4,128)} %param.13) | copy-start | bytes 6148
  18.9 15.4 %copy-start.8 = (bf16[2,100,100]{2,0,1:T(2,128)(2,1)S(1)}, bf16[2,100,100]{2,0,1:T(2,128)(2,1)}, u32[]{:S(2)}) copy-start(bf16[2,100,100]{2,0,1:T(2,128)(2,1)} %param.17) | copy-start | bytes 120004
  25.6 21.9 %copy-start.11 = (bf16[100,100]{1,0:T(8,128)(2,1)S(1)}, bf16[100,100]{1,0:T(8,128)(2,1)}, u32[]{:S(2)}) copy-start(bf16[100,100]{1,0:T(8,128)(2,1)} %param.18) | copy-start | bytes 60004
  25.6 12.5 %collective-permute-start.2 = (bf16[3,100,6,1]{3,1,2,0:T(8,128)(2,1)S(1)}, bf16[3,100,6,1]{3,1,2,0:T(8,128)(2,1)S(1)}, u32[]{:S(2)}, u32[]{:S(2)}) collective-permute-start(bf16[3,100,6,1]{3,1,2,0:T(8,128)(2,1)S(1)} %get-tuple-element.34), channel_id=1, source_target_pairs={{0,32},{32,64},{64,96},{1,33},{33,65},{65,97},{2,34},{34,66},{66,9... | collective-permute-start | bytes 10808 | tf_op jit(solution)/shard_map/ppermute | solution.py:17
  32.3 14.5 %collective-permute-start.3 = (bf16[3,100,6,1]{3,1,2,0:T(8,128)(2,1)S(1)}, bf16[3,100,6,1]{3,1,2,0:T(8,128)(2,1)S(1)}, u32[]{:S(2)}, u32[]{:S(2)}) collective-permute-start(bf16[3,100,6,1]{3,1,2,0:T(8,128)(2,1)S(1)} %get-tuple-element.35), channel_id=1, source_target_pairs={{32,0},{64,32},{96,64},{33,1},{65,33},{97,65},{34,2},{66,34},{98,6... | collective-permute-start | bytes 10808 | tf_op jit(solution)/shard_map/ppermute | solution.py:19
  47.5 10.8 %copy-start.9 = (s32[256,1]{0,1:T(1,128)S(1)}, s32[256,1]{0,1:T(1,128)}, u32[]{:S(2)}) copy-start(s32[256,1]{0,1:T(1,128)} %param.19) | copy-start | bytes 3076
  49.1 9.4 %collective-permute-start.4 = (bf16[3,100,1,128]{3,1,2,0:T(8,128)(2,1)S(1)}, bf16[3,100,1,128]{3,1,2,0:T(8,128)(2,1)S(1)}, u32[]{:S(2)}, u32[]{:S(2)}) collective-permute-start(bf16[3,100,1,128]{3,1,2,0:T(8,128)(2,1)S(1)} %get-tuple-element.42), channel_id=1, source_target_pairs={{0,1},{1,2},{2,3},{3,4},{4,5},{5,6},{6,7},{7,8},{8,9},{9,10},{10,1... | collective-permute-start | bytes 230408 | tf_op jit(solution)/shard_map/ppermute | solution.py:17
  51.0 8.7 %collective-permute-start.5 = (bf16[3,100,1,128]{3,1,2,0:T(8,128)(2,1)S(1)}, bf16[3,100,1,128]{3,1,2,0:T(8,128)(2,1)S(1)}, u32[]{:S(2)}, u32[]{:S(2)}) collective-permute-start(bf16[3,100,1,128]{3,1,2,0:T(8,128)(2,1)S(1)} %get-tuple-element.43), channel_id=1, source_target_pairs={{1,0},{2,1},{3,2},{4,3},{5,4},{6,5},{7,6},{8,7},{9,8},{10,9},{11,1... | collective-permute-start | bytes 230408 | tf_op jit(solution)/shard_map/ppermute | solution.py:19
  60.0 19.2 %collective-permute-start.6 = (bf16[3,100,6,1]{3,1,2,0:T(8,128)(2,1)S(1)}, bf16[3,100,6,1]{3,1,2,0:T(8,128)(2,1)S(1)}, u32[]{:S(2)}, u32[]{:S(2)}) collective-permute-start(bf16[3,100,6,1]{3,1,2,0:T(8,128)(2,1)S(1)} %get-tuple-element.32), channel_id=1, source_target_pairs={{0,32},{32,64},{64,96},{1,33},{33,65},{65,97},{2,34},{34,66},{66,9... | collective-permute-start | bytes 10808 | tf_op jit(solution)/shard_map/ppermute | solution.py:17
  62.9 16.3 %collective-permute-start.7 = (bf16[3,100,6,1]{3,1,2,0:T(8,128)(2,1)S(1)}, bf16[3,100,6,1]{3,1,2,0:T(8,128)(2,1)S(1)}, u32[]{:S(2)}, u32[]{:S(2)}) collective-permute-start(bf16[3,100,6,1]{3,1,2,0:T(8,128)(2,1)S(1)} %get-tuple-element.33), channel_id=1, source_target_pairs={{32,0},{64,32},{96,64},{33,1},{65,33},{97,65},{34,2},{66,34},{98,6... | collective-permute-start | bytes 10808 | tf_op jit(solution)/shard_map/ppermute | solution.py:19
  67.2 64.1 %all-to-all-start.1 = ((s32[128,1,4]{2,1,0:T(1,128)}), s32[128,1,4]{2,1,0:T(1,128)S(1)}, u32[]{:S(2)}, u32[]{:S(2)}) async-start(s32[128,1,4]{2,1,0:T(1,128)} %bitcast.22), calls=%async_computation.1 | async-start | bytes 131072 | tf_op jit(solution)/shard_map/all_to_all | solution.py:97
  79.8 11.0 %copy-start.5 = (f32[256,100]{0,1:T(8,128)S(1)}, f32[256,100]{0,1:T(8,128)}, u32[]{:S(2)}) copy-start(f32[256,100]{0,1:T(8,128)} %param.23) | copy-start | bytes 307204
  79.8 11.0 %copy-start.6 = (f32[256,100]{0,1:T(8,128)S(1)}, f32[256,100]{0,1:T(8,128)}, u32[]{:S(2)}) copy-start(f32[256,100]{0,1:T(8,128)} %param.22) | copy-start | bytes 307204
  79.8 11.0 %copy-start.7 = (f32[256,100]{0,1:T(8,128)S(1)}, f32[256,100]{0,1:T(8,128)}, u32[]{:S(2)}) copy-start(f32[256,100]{0,1:T(8,128)} %param.21) | copy-start | bytes 307204
  81.4 9.5 %collective-permute-start.8 = (bf16[3,100,1,128]{3,1,2,0:T(8,128)(2,1)S(1)}, bf16[3,100,1,128]{3,1,2,0:T(8,128)(2,1)S(1)}, u32[]{:S(2)}, u32[]{:S(2)}) collective-permute-start(bf16[3,100,1,128]{3,1,2,0:T(8,128)(2,1)S(1)} %get-tuple-element.40), channel_id=1, source_target_pairs={{0,1},{1,2},{2,3},{3,4},{4,5},{5,6},{6,7},{7,8},{8,9},{9,10},{10,1... | collective-permute-start | bytes 230408 | tf_op jit(solution)/shard_map/ppermute | solution.py:17
  84.7 7.5 %collective-permute-start.9 = (bf16[3,100,1,128]{3,1,2,0:T(8,128)(2,1)S(1)}, bf16[3,100,1,128]{3,1,2,0:T(8,128)(2,1)S(1)}, u32[]{:S(2)}, u32[]{:S(2)}) collective-permute-start(bf16[3,100,1,128]{3,1,2,0:T(8,128)(2,1)S(1)} %get-tuple-element.41), channel_id=1, source_target_pairs={{1,0},{2,1},{3,2},{4,3},{5,4},{6,5},{7,6},{8,7},{9,8},{10,9},{11,1... | collective-permute-start | bytes 230408 | tf_op jit(solution)/shard_map/ppermute | solution.py:19
  93.5 19.3 %collective-permute-start.10 = (bf16[3,100,6,1]{3,1,2,0:T(8,128)(2,1)}, bf16[3,100,6,1]{3,1,2,0:T(8,128)(2,1)S(1)}, u32[]{:S(2)}, u32[]{:S(2)}) collective-permute-start(bf16[3,100,6,1]{3,1,2,0:T(8,128)(2,1)} %get-tuple-element.30), channel_id=1, source_target_pairs={{0,32},{32,64},{64,96},{1,33},{33,65},{65,97},{2,34},{34,66},{66,9... | collective-permute-start | bytes 10808 | tf_op jit(solution)/shard_map/ppermute | solution.py:17
  102.1 17.7 %collective-permute-start.11 = (bf16[3,100,6,1]{3,1,2,0:T(8,128)(2,1)}, bf16[3,100,6,1]{3,1,2,0:T(8,128)(2,1)S(1)}, u32[]{:S(2)}, u32[]{:S(2)}) collective-permute-start(bf16[3,100,6,1]{3,1,2,0:T(8,128)(2,1)} %get-tuple-element.31), channel_id=1, source_target_pairs={{32,0},{64,32},{96,64},{33,1},{65,33},{97,65},{34,2},{66,34},{98,6... | collective-permute-start | bytes 10808 | tf_op jit(solution)/shard_map/ppermute | solution.py:19
  122.0 17.9 %collective-permute-start.12 = (bf16[3,100,1,128]{3,1,2,0:T(8,128)(2,1)S(1)}, bf16[3,100,1,128]{3,1,2,0:T(8,128)(2,1)S(1)}, u32[]{:S(2)}, u32[]{:S(2)}) collective-permute-start(bf16[3,100,1,128]{3,1,2,0:T(8,128)(2,1)S(1)} %get-tuple-element.38), channel_id=1, source_target_pairs={{0,1},{1,2},{2,3},{3,4},{4,5},{5,6},{6,7},{7,8},{8,9},{9,10},{10,1... | collective-permute-start | bytes 230408 | tf_op jit(solution)/shard_map/ppermute | solution.py:17
  124.5 15.4 %collective-permute-start.13 = (bf16[3,100,1,128]{3,1,2,0:T(8,128)(2,1)S(1)}, bf16[3,100,1,128]{3,1,2,0:T(8,128)(2,1)S(1)}, u32[]{:S(2)}, u32[]{:S(2)}) collective-permute-start(bf16[3,100,1,128]{3,1,2,0:T(8,128)(2,1)S(1)} %get-tuple-element.39), channel_id=1, source_target_pairs={{1,0},{2,1},{3,2},{4,3},{5,4},{6,5},{7,6},{8,7},{9,8},{10,9},{11,1... | collective-permute-start | bytes 230408 | tf_op jit(solution)/shard_map/ppermute | solution.py:19
  131.2 87.9 %all-to-all-start = ((f32[128,4,3,100]{3,1,2,0:T(4,128)}), f32[128,4,3,100]{3,1,2,0:T(4,128)S(1)}, u32[]{:S(2)}, u32[]{:S(2)}) async-start(f32[128,4,3,100]{3,1,2,0:T(4,128)} %copy.47), calls=%async_computation | async-start | bytes 1572864 | tf_op jit(solution)/shard_map/all_to_all | solution.py:98
  140.2 23.8 %collective-permute-start.14 = (bf16[3,100,6,1]{3,1,2,0:T(8,128)(2,1)S(1)}, bf16[3,100,6,1]{3,1,2,0:T(8,128)(2,1)S(1)}, u32[]{:S(2)}, u32[]{:S(2)}) collective-permute-start(bf16[3,100,6,1]{3,1,2,0:T(8,128)(2,1)S(1)} %get-tuple-element.28), channel_id=1, source_target_pairs={{0,32},{32,64},{64,96},{1,33},{33,65},{65,97},{2,34},{34,66},{66,9... | collective-permute-start | bytes 10808 | tf_op jit(solution)/shard_map/ppermute | solution.py:17
  147.9 26.5 %collective-permute-start.15 = (bf16[3,100,6,1]{3,1,2,0:T(8,128)(2,1)S(1)}, bf16[3,100,6,1]{3,1,2,0:T(8,128)(2,1)}, u32[]{:S(2)}, u32[]{:S(2)}) collective-permute-start(bf16[3,100,6,1]{3,1,2,0:T(8,128)(2,1)S(1)} %get-tuple-element.29), channel_id=1, source_target_pairs={{32,0},{64,32},{96,64},{33,1},{65,33},{97,65},{34,2},{66,34},{98,6... | collective-permute-start | bytes 10808 | tf_op jit(solution)/shard_map/ppermute | solution.py:19
  177.7 9.4 %collective-permute-start.16 = (bf16[3,100,1,128]{3,1,2,0:T(8,128)(2,1)S(1)}, bf16[3,100,1,128]{3,1,2,0:T(8,128)(2,1)S(1)}, u32[]{:S(2)}, u32[]{:S(2)}) collective-permute-start(bf16[3,100,1,128]{3,1,2,0:T(8,128)(2,1)S(1)} %get-tuple-element.36), channel_id=1, source_target_pairs={{0,1},{1,2},{2,3},{3,4},{4,5},{5,6},{6,7},{7,8},{8,9},{9,10},{10,1... | collective-permute-start | bytes 230408 | tf_op jit(solution)/shard_map/ppermute | solution.py:17
  180.1 8.2 %collective-permute-start.17 = (bf16[3,100,1,128]{3,1,2,0:T(8,128)(2,1)S(1)}, bf16[3,100,1,128]{3,1,2,0:T(8,128)(2,1)S(1)}, u32[]{:S(2)}, u32[]{:S(2)}) collective-permute-start(bf16[3,100,1,128]{3,1,2,0:T(8,128)(2,1)S(1)} %get-tuple-element.37), channel_id=1, source_target_pairs={{1,0},{2,1},{3,2},{4,3},{5,4},{6,5},{7,6},{8,7},{9,8},{10,9},{11,1... | collective-permute-start | bytes 230408 | tf_op jit(solution)/shard_map/ppermute | solution.py:19
  188.6 8.4 %collective-permute-start.18 = (bf16[3,100,6,1]{3,1,2,0:T(8,128)(2,1)S(1)}, bf16[3,100,6,1]{3,1,2,0:T(8,128)(2,1)S(1)}, u32[]{:S(2)}, u32[]{:S(2)}) collective-permute-start(bf16[3,100,6,1]{3,1,2,0:T(8,128)(2,1)S(1)} %get-tuple-element.26), channel_id=1, source_target_pairs={{0,32},{32,64},{64,96},{1,33},{33,65},{65,97},{2,34},{34,66},{66,9... | collective-permute-start | bytes 10808 | tf_op jit(solution)/shard_map/ppermute | solution.py:17
  191.4 17.1 %collective-permute-start.19 = (bf16[3,100,6,1]{3,1,2,0:T(8,128)(2,1)S(1)}, bf16[3,100,6,1]{3,1,2,0:T(8,128)(2,1)}, u32[]{:S(2)}, u32[]{:S(2)}) collective-permute-start(bf16[3,100,6,1]{3,1,2,0:T(8,128)(2,1)S(1)} %get-tuple-element.27), channel_id=1, source_target_pairs={{32,0},{64,32},{96,64},{33,1},{65,33},{97,65},{34,2},{66,34},{98,6... | collective-permute-start | bytes 10808 | tf_op jit(solution)/shard_map/ppermute | solution.py:19
  216.4 1.9 slice-start
  224.4 124.9 %all-to-all-start.2 = ((f32[128,4,100]{2,1,0:T(4,128)}), f32[128,4,100]{2,1,0:T(4,128)S(1)}, u32[]{:S(2)}, u32[]{:S(2)}) async-start(f32[128,4,100]{2,1,0:T(4,128)} %bitcast.35), calls=%async_computation.2 | async-start | bytes 524288 | tf_op jit(solution)/shard_map/all_to_all | solution.py:121
  (4 other events, 3.5 us)
